TPU v7x, 32 devices: a whole 2x2x4 slice. The times are simulated.
32 devices in a mesh: video: 2 (over y), space: 4 (over z), tm: 4 (over x, core).
Axes of the slice: x: 2, y: 2, z: 4, core: 2. Of those that a mesh axis runs over, the one named last changes fastest.
Arguments:
- spatial_q: bfloat16 [16, 16, 16, 1152], P(('video', 'tm'), 'space'), parts along dimension 0, may hold values from -17 to 17
- spatial_k: bfloat16 [16, 16, 16, 1152], P(('video', 'tm'), 'space'), parts along dimension 0, may hold values from -17 to 17
- spatial_v: bfloat16 [16, 16, 16, 1152], P(('video', 'tm'), 'space'), parts along dimension 0, may hold values from -6 to 6
- temporal_q: bfloat16 [16, 16, 16, 1152], P(('video', 'tm'), 'space'), parts along dimension 0, may hold values from -17 to 17
- temporal_k: bfloat16 [16, 16, 16, 1152], P(('video', 'tm'), 'space'), parts along dimension 0, may hold values from -17 to 17
- temporal_v: bfloat16 [16, 16, 16, 1152], P(('video', 'tm'), 'space'), parts along dimension 0, may hold values from -6 to 6
- key_lists: int32 [16, 8], replicated, may hold values from -1 to 15, as said below
Outputs:
- spatial_out: bfloat16 [16, 16, 16, 1152], P(('video', 'tm'), 'space'), parts along dimension 0
- temporal_out: bfloat16 [16, 16, 16, 1152], P(('video', 'tm'), 'space'), parts along dimension 0
There are 2 independent parts, one for each index of `video`. A program takes and returns all parts, laid end to end along the dimension named above; an argument that names none is the same for every part. Nothing has to cross between parts.
Inputs may be any that keep to these rules, and one draw needn't show every extreme that they name: key_lists[r] names distinct tile rows within 4 rows of r, r itself first; the named entries come first and the rest are -1.
All inputs are finite; a program needn't handle non-finite values.
Results may differ from a plain program's by a relative error of at most 0.0037.
Values may be sent and summed in bfloat16 or wider, within the bound.
A program may use at most 64 MiB of HBM per device.

v0:
```python
import functools
import math

import jax
import jax.numpy as jnp
from jax import lax
from jax.experimental import pallas as pl
from jax.experimental.pallas import tpu as pltpu
from jax.sharding import PartitionSpec as P

HEAD_DIM = 72
LANES = 128
BIG_NEGATIVE = -1e30
MESH = pl.DeviceIdType.MESH


def head_windows(channels):
    heads = channels // HEAD_DIM
    groups = []
    h = 0
    while h < heads:
        base = (h * HEAD_DIM) // LANES
        base = min(base, channels // LANES - 2)
        group = []
        while h < heads and (h + 1) * HEAD_DIM <= (base + 2) * LANES:
            group.append(h)
            h += 1
        groups.append((base, group))
    return groups


CUTS = (5, 7)


def chunk_tiles(tiles):
    edges = [0] + [c for c in CUTS if c < tiles] + [tiles]
    return list(zip(edges[:-1], edges[1:]))


def flipped(index, j):
    bit = 1
    while bit <= j:
        if j & bit:
            index = index + bit - 2 * bit * ((index // bit) % 2)
        bit *= 2
    return index


def attend(problems):
    factor = HEAD_DIM ** (-0.5) * math.log2(math.e)
    insides = []
    scored = []
    for (base, group), load_q, load_k, _, _, bias, queries in problems:
        lane = lax.broadcasted_iota(jnp.int32, (queries, 2 * LANES), 1)
        q = load_q(base)
        inside = []
        for h in group:
            low = h * HEAD_DIM - base * LANES
            inside.append((lane >= low) & (lane < low + HEAD_DIM))
        stack = jnp.concatenate(
            [jnp.where(m, q, jnp.zeros_like(q)) for m in inside], axis=0
        )
        scores = lax.dot_general(
            stack, load_k(base), (((1,), (1,)), ((), ())), preferred_element_type=jnp.float32
        )
        scored.append(scores.reshape(len(group), queries, -1) * factor + bias[...][None])
        insides.append(inside)
    weighed = []
    for scores in scored:
        highest = jnp.max(scores, axis=-1, keepdims=True)
        weights = jnp.exp2(scores - highest)
        totals = jnp.sum(weights, axis=-1, keepdims=True)
        rounded = weights.astype(jnp.bfloat16).reshape(-1, weights.shape[-1])
        weighed.append((rounded, 1.0 / totals))
    for ((base, group), _, _, load_v, store, _, queries), (rounded, inverse), inside in zip(
        problems, weighed, insides
    ):
        blended = jnp.dot(rounded, load_v(base), preferred_element_type=jnp.float32)
        blended = blended.reshape(len(group), queries, 2 * LANES) * inverse
        merged = jnp.zeros((queries, 2 * LANES), jnp.float32)
        for n, m in enumerate(inside):
            merged = jnp.where(m, blended[n], merged)
        store(merged)


def kernel(
    space_count, tm_count, reach,
    sq, sk, sv, tq, tk, tv, lists, sov, tov,
    sqv, kwin, vwin, tqv, tkb, tvb, sbias, tbias, entry,
    zsend, zrecv, xsend, xrecv, load_sem,
):
    frames, rows, cols, channels = sqv.shape
    s = lax.axis_index("space")
    t = lax.axis_index("tm")
    entries = lists.shape[0]
    extent = (2 * reach + 1) * rows
    groups = head_windows(channels)
    tiles = channels // LANES
    chunks = chunk_tiles(tiles)
    needed_last = [
        max(c for c in range(len(chunks)) if chunks[c][0] < base + 2) for base, _ in groups
    ]

    direct = [1] + list(range(2, tm_count, 2))
    z_moves = []
    for d in range(1, reach + 1):
        z_moves.append((d, reach - d, 2 * (d - 1)))
        z_moves.append((-d, reach + d, 2 * (d - 1) + 1))

    def lanes(c):
        low, high = chunks[c]
        return pl.ds(low * LANES, (high - low) * LANES)

    def reaches(by):
        return s + by < space_count if by > 0 else s + by >= 0

    def z_copy(which, c, move):
        by, place, index = move
        src = (sk, sv)[which]
        dst = (kwin, vwin)[which]
        return pltpu.make_async_remote_copy(
            src_ref=src.at[:, :, :, lanes(c)],
            dst_ref=dst.at[:, pl.ds(place * rows, rows), :, lanes(c)],
            send_sem=zsend.at[which, c, index],
            recv_sem=zrecv.at[which, c, index],
            device_id={"space": s + by},
            device_id_type=MESH,
        )

    def x_copy(which, c, j):
        dst = (tkb, tvb)[which]
        if j in direct:
            src = (tk, tv)[which].at[:, :, :, lanes(c)]
            peer = flipped(t, j)
        else:
            src = dst.at[pl.ds((j - 1) * frames, frames), :, :, lanes(c)]
            peer = flipped(t, 1)
        return pltpu.make_async_remote_copy(
            src_ref=src,
            dst_ref=dst.at[pl.ds(j * frames, frames), :, :, lanes(c)],
            send_sem=xsend.at[which, c, j],
            recv_sem=xrecv.at[which, c, j],
            device_id={"tm": peer},
            device_id_type=MESH,
        )

    loads = []
    middle = pl.ds(reach * rows, rows)
    for n, (src, dst) in enumerate(
        [
            (tq, tqv),
            (tk, tkb.at[pl.ds(0, frames)]),
            (tv, tvb.at[pl.ds(0, frames)]),
            (sq, sqv),
            (sk, kwin.at[:, middle]),
            (sv, vwin.at[:, middle]),
            (lists, entry),
        ]
    ):
        loads.append(pltpu.make_async_copy(src, dst, load_sem.at[n]))

    barrier = pltpu.get_barrier_semaphore()
    for j in direct:
        pl.semaphore_signal(
            barrier, inc=1, device_id={"tm": flipped(t, j)}, device_id_type=MESH
        )
    peers = len(direct)
    for by, _, _ in z_moves:
        peers = peers + jnp.where(reaches(by), 1, 0)

        @pl.when(reaches(by))
        def _():
            pl.semaphore_signal(
                barrier, inc=1, device_id={"space": s + by}, device_id_type=MESH
            )
    for copy in loads:
        copy.start()
    pl.semaphore_wait(barrier, peers)

    for c in range(len(chunks)):
        for which in (0, 1):
            for j in direct[1:] + direct[:1]:
                x_copy(which, c, j).start()
    for move in z_moves:
        @pl.when(reaches(move[0]))
        def _():
            for c in range(len(chunks)):
                for which in (0, 1):
                    z_copy(which, c, move).start()

    for by, place, _ in z_moves:
        @pl.when(jnp.logical_not(reaches(-by)))
        def _():
            zeros = jnp.zeros((frames, rows, cols, channels), jnp.bfloat16)
            kwin[:, pl.ds(place * rows, rows)] = zeros
            vwin[:, pl.ds(place * rows, rows)] = zeros

    loads.pop().wait()
    column = lax.broadcasted_iota(jnp.int32, (cols, extent * cols), 1)
    for i in range(rows):
        member = jnp.zeros((cols, extent * cols), jnp.float32) + BIG_NEGATIVE
        for e in range(entries):
            row = entry[e, s * rows + i]
            low = (row - (s - reach) * rows) * cols
            low = jnp.where(row >= 0, low, -extent * cols)
            member = jnp.where((column >= low) & (column < low + cols), 0.0, member)
        sbias[pl.ds(i * cols, cols)] = member
    shape = tbias.shape
    tbias[...] = jnp.where(
        lax.broadcasted_iota(jnp.int32, shape, 0) % cols
        == lax.broadcasted_iota(jnp.int32, shape, 1) % cols,
        0.0,
        BIG_NEGATIVE,
    )
    for copy in loads:
        copy.wait()

    def pair(base):
        return slice(base * LANES, (base + 2) * LANES)

    pending = {}

    def keep(name, number, merged, put):
        base = groups[number][0]
        upcoming = groups[number + 1][0] if number + 1 < len(groups) else tiles
        for tile in (base, base + 1):
            part = merged[:, (tile - base) * LANES : (tile - base + 1) * LANES]
            if (name, tile) in pending:
                part = pending.pop((name, tile)) + part
            if tile < upcoming:
                put(slice(tile * LANES, (tile + 1) * LANES), part.astype(jnp.bfloat16))
            else:
                pending[name, tile] = part

    def spatial(number, f):
        def store(merged):
            def put(where, value):
                sov[f, :, :, where] = value.reshape(rows, cols, LANES)

            keep(("s", f), number, merged, put)

        return (
            groups[number],
            lambda b: sqv[f, :, :, pair(b)].reshape(rows * cols, 2 * LANES),
            lambda b: kwin[f, :, :, pair(b)].reshape(extent * cols, 2 * LANES),
            lambda b: vwin[f, :, :, pair(b)].reshape(extent * cols, 2 * LANES),
            store, sbias, rows * cols,
        )

    def temporal(number, r):
        def store(merged):
            def put(where, value):
                tov[:, r, :, where] = value.reshape(frames, cols, LANES)

            keep(("t", r), number, merged, put)

        keys = tm_count * frames * cols
        return (
            groups[number],
            lambda b: tqv[:, r, :, pair(b)].reshape(frames * cols, 2 * LANES),
            lambda b: tkb[:, r, :, pair(b)].reshape(keys, 2 * LANES),
            lambda b: tvb[:, r, :, pair(b)].reshape(keys, 2 * LANES),
            store, tbias, frames * cols,
        )

    ready = [[g for g in range(len(groups)) if needed_last[g] == c] for c in range(len(chunks))]
    for c in range(len(chunks) + 1):
        if c < len(chunks):
            for j in direct[1:]:
                for which in (0, 1):
                    x_copy(which, c, j).wait_recv()
                    x_copy(which, c, j + 1).start()
            for move in z_moves:
                @pl.when(reaches(-move[0]))
                def _():
                    for which in (0, 1):
                        z_copy(which, c, move).wait_recv()
        near = ready[c] if c < len(chunks) else []
        far = ready[c - 1] if c > 0 else []
        for at in range(0, max(len(near), len(far)), 2):
            problems = [spatial(g, f) for g in near[at : at + 2] for f in range(frames)]
            if c > 0 and at == 0:
                for j in [1] + [j + 1 for j in direct[1:]]:
                    for which in (0, 1):
                        x_copy(which, c - 1, j).wait_recv()
            problems += [temporal(g, r) for g in far[at : at + 2] for r in range(rows)]
            attend(problems)

    for c in range(len(chunks)):
        for which in (0, 1):
            for j in range(1, tm_count):
                x_copy(which, c, j).wait_send()
    for move in z_moves:
        @pl.when(reaches(move[0]))
        def _():
            for c in range(len(chunks)):
                for which in (0, 1):
                    z_copy(which, c, move).wait_send()


def written(first, second, first_out, second_out, sem):
    copies = [
        pltpu.make_async_copy(first, first_out, sem.at[0]),
        pltpu.make_async_copy(second, second_out, sem.at[1]),
    ]
    for copy in copies:
        copy.start()
    for copy in copies:
        copy.wait()


def on_device(space_count, tm_count, sq, sk, sv, tq, tk, tv, lists):
    frames, rows, cols, channels = sq.shape
    reach = min(5, (space_count - 1) // 2)
    extent = (2 * reach + 1) * rows
    block = (frames, rows, cols, channels)
    window = (frames, extent, cols, channels)
    gathered = (tm_count * frames, rows, cols, channels)
    pieces = len(chunk_tiles(channels // LANES))
    bf16 = jnp.bfloat16
    any_spec = pl.BlockSpec(memory_space=pl.ANY)
    dma = pltpu.SemaphoreType.DMA
    results = pl.pallas_call(
        functools.partial(kernel, space_count, tm_count, reach),
        out_shape=(pltpu.VMEM(block, bf16), pltpu.VMEM(block, bf16)),
        in_specs=[any_spec] * 7,
        out_specs=(pl.BlockSpec(memory_space=pltpu.VMEM),) * 2,
        scratch_shapes=[
            pltpu.VMEM(block, bf16),
            pltpu.VMEM(window, bf16),
            pltpu.VMEM(window, bf16),
            pltpu.VMEM(block, bf16),
            pltpu.VMEM(gathered, bf16),
            pltpu.VMEM(gathered, bf16),
            pltpu.VMEM((rows * cols, extent * cols), jnp.float32),
            pltpu.VMEM((frames * cols, tm_count * frames * cols), jnp.float32),
            pltpu.SMEM(lists.shape[::-1], jnp.int32),
            dma((2, pieces, 2 * reach)),
            dma((2, pieces, 2 * reach)),
            dma((2, pieces, tm_count)),
            dma((2, pieces, tm_count)),
            dma((7,)),
        ],
        compiler_params=pltpu.CompilerParams(collective_id=0, has_side_effects=True),
        name="attention",
    )(sq, sk, sv, tq, tk, tv, lists.T)
    return pl.pallas_call(
        written,
        out_shape=(jax.ShapeDtypeStruct(block, bf16), jax.ShapeDtypeStruct(block, bf16)),
        in_specs=[any_spec] * 2,
        out_specs=(any_spec, any_spec),
        scratch_shapes=[dma((2,))],
        name="written",
    )(*[pltpu.with_memory_space_constraint(x, pltpu.VMEM) for x in results])


def solution(mesh):
    block = P(("video", "tm"), "space", None, None)
    return jax.shard_map(
        functools.partial(on_device, mesh.shape["space"], mesh.shape["tm"]),
        mesh=mesh,
        in_specs=(block,) * 6 + (P(),),
        out_specs=(block, block),
        check_vma=False,
    )
```

profile of v0, /device:TPU:0, one launch (start us, length us, event | category | flops | bytes accessed | tf_op | source)
XLA Modules:
  0.0 21.4 jit_solution(18192269486091863856)
XLA Ops:
  0.6 20.0 %attention.1 = (bf16[2,4,16,1152]{3,2,1,0:T(8,128)(2,1)S(1)}, bf16[2,4,16,1152]{3,2,1,0:T(8,128)(2,1)S(1)}) custom-call(bf16[2,4,16,1152]{3,2,1,0:T(8,128)(2,1)} %sq.1, bf16[2,4,16,1152]{3,2,1,0:T(8,128)(2,1)} %sk.1, bf16[2,4,16,1152]{3,2,1,0:T(8,128)(2,1)} %sv.1, bf16[2,4,16,1152]{3,2,1,0:T(8,128)(2,1)} %tq.1, bf16[2,4,16,1152]{3,2,1,0:T(8,128)(2,1)} %tk.1, ...), custom_call_target="tpu_custom_call" | custom-call | tf_op jit(solution)/shard_map/attention/pallas_call | solution.py:323
  20.6 0.8 %written.1 = (bf16[2,4,16,1152]{3,2,1,0:T(8,128)(2,1)}, bf16[2,4,16,1152]{3,2,1,0:T(8,128)(2,1)}) custom-call(bf16[2,4,16,1152]{3,2,1,0:T(8,128)(2,1)S(1)} %get-tuple-element.4.first, bf16[2,4,16,1152]{3,2,1,0:T(8,128)(2,1)S(1)} %get-tuple-element.5.second), custom_call_target="tpu_custom_call" | custom-call | tf_op jit(solution)/shard_map/written/pallas_call | solution.py:347
where the time goes:
time: 21.6 us; the launch traced here: 21.4 us
  Pallas kernels  20.8 us (96%)
  between operations  0.64 us (3%)
    pallas_call x1, Pallas kernels, on_device(): pl.pallas_call(functools.partial(kernel, space_count, tm_count, reach), o...  20 us
    pallas_call x1, Pallas kernels, on_device(): pl.pallas_call(written, out_shape=(jax.ShapeDtypeStruct(block, bf16), jax...  0.83 us

commit v1 on v0

--- a/solution.py
+++ b/solution.py
@@ -87,7 +87,7 @@
     space_count, tm_count, reach,
     sq, sk, sv, tq, tk, tv, lists, sov, tov,
     sqv, kwin, vwin, tqv, tkb, tvb, sbias, tbias, entry,
-    zsend, zrecv, xsend, xrecv, load_sem,
+    zsend, zrecv, xsend, xrecv, zready, xready, load_sem,
 ):
     frames, rows, cols, channels = sqv.shape
     s = lax.axis_index("space")
@@ -159,34 +159,72 @@
     ):
         loads.append(pltpu.make_async_copy(src, dst, load_sem.at[n]))
 
+    def above(j):
+        return flipped(t, j) > t
+
+    def tell(semaphore, peer):
+        pl.semaphore_signal(semaphore, inc=1, device_id=peer, device_id_type=MESH)
+
     barrier = pltpu.get_barrier_semaphore()
+    peers = 0
     for j in direct:
-        pl.semaphore_signal(
-            barrier, inc=1, device_id={"tm": flipped(t, j)}, device_id_type=MESH
-        )
-    peers = len(direct)
-    for by, _, _ in z_moves:
-        peers = peers + jnp.where(reaches(by), 1, 0)
-
-        @pl.when(reaches(by))
-        def _():
-            pl.semaphore_signal(
-                barrier, inc=1, device_id={"space": s + by}, device_id_type=MESH
-            )
+        peers = peers + jnp.where(above(j), 0, 1)
+
+        @pl.when(above(j))
+        def _():
+            tell(barrier, {"tm": flipped(t, j)})
+    for d in range(1, reach + 1):
+        peers = peers + jnp.where(reaches(-d), 1, 0)
+
+        @pl.when(reaches(d))
+        def _():
+            tell(barrier, {"space": s + d})
     for copy in loads:
         copy.start()
-    pl.semaphore_wait(barrier, peers)
-
-    for c in range(len(chunks)):
-        for which in (0, 1):
-            for j in direct[1:] + direct[:1]:
+
+    @pl.when(peers > 0)
+    def _():
+        pl.semaphore_wait(barrier, peers)
+
+    def send_x(j):
+        for c in range(len(chunks)):
+            for which in (0, 1):
                 x_copy(which, c, j).start()
+
+    def send_z(move):
+        for c in range(len(chunks)):
+            for which in (0, 1):
+                z_copy(which, c, move).start()
+
+    for d in range(1, reach + 1):
+        @pl.when(reaches(-d))
+        def _():
+            tell(zready.at[d - 1], {"space": s - d})
+    for j in direct:
+        @pl.when(jnp.logical_not(above(j)))
+        def _():
+            tell(xready.at[j], {"tm": flipped(t, j)})
+    outward = direct[1:] + direct[:1]
     for move in z_moves:
-        @pl.when(reaches(move[0]))
-        def _():
-            for c in range(len(chunks)):
-                for which in (0, 1):
-                    z_copy(which, c, move).start()
+        if move[0] < 0:
+            @pl.when(reaches(move[0]))
+            def _():
+                send_z(move)
+    for j in outward:
+        @pl.when(jnp.logical_not(above(j)))
+        def _():
+            send_x(j)
+    for j in outward:
+        @pl.when(above(j))
+        def _():
+            pl.semaphore_wait(xready.at[j], 1)
+            send_x(j)
+    for move in z_moves:
+        if move[0] > 0:
+            @pl.when(reaches(move[0]))
+            def _():
+                pl.semaphore_wait(zready.at[move[0] - 1], 1)
+                send_z(move)
 
     for by, place, _ in z_moves:
         @pl.when(jnp.logical_not(reaches(-by)))
@@ -339,6 +377,8 @@
             dma((2, pieces, 2 * reach)),
             dma((2, pieces, tm_count)),
             dma((2, pieces, tm_count)),
+            pltpu.SemaphoreType.REGULAR((max(reach, 1),)),
+            pltpu.SemaphoreType.REGULAR((tm_count,)),
             dma((7,)),
         ],
         compiler_params=pltpu.CompilerParams(collective_id=0, has_side_effects=True),

time: 21.6 us -> 21 us (0.972)
  Pallas kernels: 20.8 us -> 20.2 us
    pallas_call x1, Pallas kernels: 20 us -> 19.3 us  [on_device(): pl.pallas_call(functools.partial(kernel, space_count, tm_count, reach), o...]
where the time goes in v1:
time: 21 us; the launch traced here: 20.8 us
  Pallas kernels  20.2 us (96%)
  between operations  0.64 us (3%)
    pallas_call x1, Pallas kernels, on_device(): pl.pallas_call(functools.partial(kernel, space_count, tm_count, reach), o...  19.3 us
    pallas_call x1, Pallas kernels, on_device(): pl.pallas_call(written, out_shape=(jax.ShapeDtypeStruct(block, bf16), jax...  0.83 us

profile of v1, /device:TPU:0, one launch (start us, length us, event | category | flops | bytes accessed | tf_op | source)
XLA Modules:
  0.0 20.8 jit_solution(12208379325458855883)
XLA Ops:
  0.6 19.3 %attention.1 = (bf16[2,4,16,1152]{3,2,1,0:T(8,128)(2,1)S(1)}, bf16[2,4,16,1152]{3,2,1,0:T(8,128)(2,1)S(1)}) custom-call(bf16[2,4,16,1152]{3,2,1,0:T(8,128)(2,1)} %sq.1, bf16[2,4,16,1152]{3,2,1,0:T(8,128)(2,1)} %sk.1, bf16[2,4,16,1152]{3,2,1,0:T(8,128)(2,1)} %sv.1, bf16[2,4,16,1152]{3,2,1,0:T(8,128)(2,1)} %tq.1, bf16[2,4,16,1152]{3,2,1,0:T(8,128)(2,1)} %tk.1, ...), custom_call_target="tpu_custom_call" | custom-call | tf_op jit(solution)/shard_map/attention/pallas_call | solution.py:361
  20.0 0.8 %written.1 = (bf16[2,4,16,1152]{3,2,1,0:T(8,128)(2,1)}, bf16[2,4,16,1152]{3,2,1,0:T(8,128)(2,1)}) custom-call(bf16[2,4,16,1152]{3,2,1,0:T(8,128)(2,1)S(1)} %get-tuple-element.4.first, bf16[2,4,16,1152]{3,2,1,0:T(8,128)(2,1)S(1)} %get-tuple-element.5.second), custom_call_target="tpu_custom_call" | custom-call | tf_op jit(solution)/shard_map/written/pallas_call | solution.py:387

commit v2 on v1

--- a/solution.py
+++ b/solution.py
@@ -29,12 +29,16 @@
     return groups
 
 
-CUTS = (5, 7)
+CUTS = (5, 8)
 
 
 def chunk_tiles(tiles):
     edges = [0] + [c for c in CUTS if c < tiles] + [tiles]
     return list(zip(edges[:-1], edges[1:]))
+
+
+def kept_rows(rows, tm_count):
+    return rows - 1 if rows > 1 and tm_count > 2 else rows
 
 
 def flipped(index, j):
@@ -46,11 +50,11 @@
     return index
 
 
-def attend(problems):
+def attend(problems, between=None):
     factor = HEAD_DIM ** (-0.5) * math.log2(math.e)
     insides = []
     scored = []
-    for (base, group), load_q, load_k, _, _, bias, queries in problems:
+    for (base, group), load_q, load_k, _, _, bias, queries, _ in problems:
         lane = lax.broadcasted_iota(jnp.int32, (queries, 2 * LANES), 1)
         q = load_q(base)
         inside = []
@@ -66,13 +70,17 @@
         scored.append(scores.reshape(len(group), queries, -1) * factor + bias[...][None])
         insides.append(inside)
     weighed = []
-    for scores in scored:
+    for scores, (_, _, _, _, _, _, _, note) in zip(scored, problems):
         highest = jnp.max(scores, axis=-1, keepdims=True)
         weights = jnp.exp2(scores - highest)
         totals = jnp.sum(weights, axis=-1, keepdims=True)
         rounded = weights.astype(jnp.bfloat16).reshape(-1, weights.shape[-1])
         weighed.append((rounded, 1.0 / totals))
-    for ((base, group), _, _, load_v, store, _, queries), (rounded, inverse), inside in zip(
+        if note is not None:
+            note(highest + jnp.log(totals) * math.log2(math.e))
+    if between is not None:
+        between()
+    for ((base, group), _, _, load_v, store, _, queries, _), (rounded, inverse), inside in zip(
         problems, weighed, insides
     ):
         blended = jnp.dot(rounded, load_v(base), preferred_element_type=jnp.float32)
@@ -87,13 +95,15 @@
     space_count, tm_count, reach,
     sq, sk, sv, tq, tk, tv, lists, sov, tov,
     sqv, kwin, vwin, tqv, tkb, tvb, sbias, tbias, entry,
-    zsend, zrecv, xsend, xrecv, zready, xready, load_sem,
+    asked, answer, answered, own, spread,
+    zsend, zrecv, xsend, xrecv, qsend, qrecv, osend, orecv, zready, xready, load_sem,
 ):
     frames, rows, cols, channels = sqv.shape
     s = lax.axis_index("space")
     t = lax.axis_index("tm")
     entries = lists.shape[0]
     extent = (2 * reach + 1) * rows
+    heads = channels // HEAD_DIM
     groups = head_windows(channels)
     tiles = channels // LANES
     chunks = chunk_tiles(tiles)
@@ -102,6 +112,8 @@
     ]
 
     direct = [1] + list(range(2, tm_count, 2))
+    kept = kept_rows(rows, tm_count)
+    lent = direct[1:] if kept < rows else []
     z_moves = []
     for d in range(1, reach + 1):
         z_moves.append((d, reach - d, 2 * (d - 1)))
@@ -129,18 +141,39 @@
 
     def x_copy(which, c, j):
         dst = (tkb, tvb)[which]
+        here = pl.ds(0, rows if j == 1 else kept)
         if j in direct:
-            src = (tk, tv)[which].at[:, :, :, lanes(c)]
+            src = (tk, tv)[which].at[:, here, :, lanes(c)]
             peer = flipped(t, j)
         else:
-            src = dst.at[pl.ds((j - 1) * frames, frames), :, :, lanes(c)]
+            src = dst.at[pl.ds((j - 1) * frames, frames), here, :, lanes(c)]
             peer = flipped(t, 1)
         return pltpu.make_async_remote_copy(
             src_ref=src,
-            dst_ref=dst.at[pl.ds(j * frames, frames), :, :, lanes(c)],
+            dst_ref=dst.at[pl.ds(j * frames, frames), here, :, lanes(c)],
             send_sem=xsend.at[which, c, j],
             recv_sem=xrecv.at[which, c, j],
             device_id={"tm": peer},
+            device_id_type=MESH,
+        )
+
+    def q_copy(n):
+        return pltpu.make_async_remote_copy(
+            src_ref=tq.at[:, pl.ds(kept, 1)],
+            dst_ref=asked.at[n],
+            send_sem=qsend.at[n],
+            recv_sem=qrecv.at[n],
+            device_id={"tm": flipped(t, lent[n])},
+            device_id_type=MESH,
+        )
+
+    def o_copy(n):
+        return pltpu.make_async_remote_copy(
+            src_ref=answer.at[n],
+            dst_ref=answered.at[n],
+            send_sem=osend.at[n],
+            recv_sem=orecv.at[n],
+            device_id={"tm": flipped(t, lent[n])},
             device_id_type=MESH,
         )
 
@@ -187,6 +220,8 @@
         pl.semaphore_wait(barrier, peers)
 
     def send_x(j):
+        if j in lent:
+            q_copy(lent.index(j)).start()
         for c in range(len(chunks)):
             for which in (0, 1):
                 x_copy(which, c, j).start()
@@ -204,7 +239,7 @@
         @pl.when(jnp.logical_not(above(j)))
         def _():
             tell(xready.at[j], {"tm": flipped(t, j)})
-    outward = direct[1:] + direct[:1]
+    outward = direct
     for move in z_moves:
         if move[0] < 0:
             @pl.when(reaches(move[0]))
@@ -250,6 +285,12 @@
         0.0,
         BIG_NEGATIVE,
     )
+    if lent:
+        row = lax.broadcasted_iota(jnp.int32, spread.shape, 0)
+        low = lax.broadcasted_iota(jnp.int32, spread.shape, 1) - (row % heads) * HEAD_DIM
+        spread[...] = jnp.where(
+            (low >= 0) & (low < HEAD_DIM) & (row < 3 * heads), 1.0, 0.0
+        ).astype(jnp.bfloat16)
     for copy in loads:
         copy.wait()
 
@@ -266,14 +307,14 @@
             if (name, tile) in pending:
                 part = pending.pop((name, tile)) + part
             if tile < upcoming:
-                put(slice(tile * LANES, (tile + 1) * LANES), part.astype(jnp.bfloat16))
+                put(slice(tile * LANES, (tile + 1) * LANES), part)
             else:
                 pending[name, tile] = part
 
     def spatial(number, f):
         def store(merged):
             def put(where, value):
-                sov[f, :, :, where] = value.reshape(rows, cols, LANES)
+                sov[f, :, :, where] = value.astype(jnp.bfloat16).reshape(rows, cols, LANES)
 
             keep(("s", f), number, merged, put)
 
@@ -282,13 +323,13 @@
             lambda b: sqv[f, :, :, pair(b)].reshape(rows * cols, 2 * LANES),
             lambda b: kwin[f, :, :, pair(b)].reshape(extent * cols, 2 * LANES),
             lambda b: vwin[f, :, :, pair(b)].reshape(extent * cols, 2 * LANES),
-            store, sbias, rows * cols,
+            store, sbias, rows * cols, None,
         )
 
     def temporal(number, r):
         def store(merged):
             def put(where, value):
-                tov[:, r, :, where] = value.reshape(frames, cols, LANES)
+                tov[:, r, :, where] = value.astype(jnp.bfloat16).reshape(frames, cols, LANES)
 
             keep(("t", r), number, merged, put)
 
@@ -298,32 +339,133 @@
             lambda b: tqv[:, r, :, pair(b)].reshape(frames * cols, 2 * LANES),
             lambda b: tkb[:, r, :, pair(b)].reshape(keys, 2 * LANES),
             lambda b: tvb[:, r, :, pair(b)].reshape(keys, 2 * LANES),
-            store, tbias, frames * cols,
-        )
+            store, tbias, frames * cols, None,
+        )
+
+    tokens = frames * cols
+    lane = lax.broadcasted_iota(jnp.int32, (tokens, LANES), 1)
+    sums = {}
+
+    def part(number, n):
+        def store(merged):
+            def put(where, value):
+                if n < 0:
+                    own[:, where] = value
+                else:
+                    value = value.astype(jnp.bfloat16)
+                    answer[n, :, :, :, where] = value.reshape(frames, 1, cols, LANES)
+
+            keep(("p", n), number, merged, put)
+
+        def note(logs):
+            known = sums.get(n, jnp.zeros((tokens, LANES), jnp.float32))
+            for at, h in enumerate(groups[number][1]):
+                known = jnp.where((lane % heads) == h, logs[at], known)
+            sums[n] = known
+
+        def load_q(b):
+            if n < 0:
+                return tqv[:, kept, :, pair(b)].reshape(tokens, 2 * LANES)
+            return asked[n, :, :, :, pair(b)].reshape(tokens, 2 * LANES)
+
+        return (
+            groups[number], load_q,
+            lambda b: tkb[: 2 * frames, kept, :, pair(b)].reshape(2 * tokens, 2 * LANES),
+            lambda b: tvb[: 2 * frames, kept, :, pair(b)].reshape(2 * tokens, 2 * LANES),
+            store, tbias.at[:, : 2 * tokens], tokens, note,
+        )
+
+    def three(total):
+        first = total.astype(jnp.bfloat16)
+        rest = total - first.astype(jnp.float32)
+        second = rest.astype(jnp.bfloat16)
+        third = (rest - second.astype(jnp.float32)).astype(jnp.bfloat16)
+        none = jnp.zeros_like(first)
+        terms = jnp.where(lane < 2 * heads, second, jnp.where(lane < 3 * heads, third, none))
+        return jnp.where(lane < heads, first, terms)
+
+    def wait_direct(c):
+        for j in direct[1:]:
+            for which in (0, 1):
+                x_copy(which, c, j).wait_recv()
+                x_copy(which, c, j + 1).start()
+
+    def wait_relayed(c):
+        for j in direct[1:]:
+            for which in (0, 1):
+                x_copy(which, c, j + 1).wait_recv()
+
+    def wait_z(c, which):
+        for move in z_moves:
+            @pl.when(reaches(-move[0]))
+            def _():
+                z_copy(which, c, move).wait_recv()
 
     ready = [[g for g in range(len(groups)) if needed_last[g] == c] for c in range(len(chunks))]
-    for c in range(len(chunks) + 1):
-        if c < len(chunks):
-            for j in direct[1:]:
-                for which in (0, 1):
-                    x_copy(which, c, j).wait_recv()
-                    x_copy(which, c, j + 1).start()
-            for move in z_moves:
-                @pl.when(reaches(-move[0]))
-                def _():
-                    for which in (0, 1):
-                        z_copy(which, c, move).wait_recv()
-        near = ready[c] if c < len(chunks) else []
-        far = ready[c - 1] if c > 0 else []
-        for at in range(0, max(len(near), len(far)), 2):
-            problems = [spatial(g, f) for g in near[at : at + 2] for f in range(frames)]
-            if c > 0 and at == 0:
-                for j in [1] + [j + 1 for j in direct[1:]]:
-                    for which in (0, 1):
-                        x_copy(which, c - 1, j).wait_recv()
-            problems += [temporal(g, r) for g in far[at : at + 2] for r in range(rows)]
-            attend(problems)
-
+
+    def across(c):
+        wait_z(c, 0)
+        for at in range(0, len(ready[c]), 2):
+            problems = [spatial(g, f) for g in ready[c][at : at + 2] for f in range(frames)]
+            attend(problems, functools.partial(wait_z, c, 1) if at == 0 else None)
+
+    def along(c):
+        wait_relayed(c)
+        for at in range(0, len(ready[c]), 2):
+            attend([temporal(g, r) for g in ready[c][at : at + 2] for r in range(kept)])
+
+    for c in range(len(chunks)):
+        for which in (0, 1):
+            x_copy(which, c, 1).wait_recv()
+    if lent:
+        for n in range(len(lent)):
+            q_copy(n).wait_recv()
+        for at in range(0, len(groups), 2):
+            numbers = range(at, min(at + 2, len(groups)))
+            attend([part(g, n) for g in numbers for n in range(-1, len(lent))])
+        for n in range(len(lent)):
+            terms = three(sums[n]).reshape(frames, 1, cols, LANES)
+            answer[n, :, :, :, channels:] = terms
+        own_terms = three(sums[-1])
+
+    def return_parts():
+        for n in range(len(lent)):
+            o_copy(n).start()
+
+    last = len(chunks) - 1
+    for c in range(len(chunks)):
+        wait_direct(c)
+        if c == max(last - 1, 0):
+            return_parts()
+        if c < last - 1:
+            across(c)
+        if c == last and c > 0:
+            across(c - 1)
+        along(c)
+    across(last)
+
+    if lent:
+        for n in range(len(lent)):
+            o_copy(n).wait_recv()
+
+        def spread_out(terms):
+            return jnp.dot(terms, spread[...], preferred_element_type=jnp.float32)
+
+        logs = [spread_out(own_terms)]
+        parts = [own[...]]
+        for n in range(len(lent)):
+            logs.append(spread_out(answered[n, :, :, :, channels:].reshape(tokens, LANES)))
+            value = answered[n, :, :, :, :channels].reshape(tokens, channels)
+            parts.append(value.astype(jnp.float32))
+        highest = functools.reduce(jnp.maximum, logs)
+        weights = [jnp.exp2(log - highest) for log in logs]
+        total = functools.reduce(jnp.add, weights)
+        mixed = functools.reduce(jnp.add, [w * p for w, p in zip(weights, parts)]) / total
+        tov[:, kept] = mixed.astype(jnp.bfloat16).reshape(frames, cols, channels)
+
+    for n in range(len(lent)):
+        q_copy(n).wait_send()
+        o_copy(n).wait_send()
     for c in range(len(chunks)):
         for which in (0, 1):
             for j in range(1, tm_count):
@@ -355,6 +497,7 @@
     window = (frames, extent, cols, channels)
     gathered = (tm_count * frames, rows, cols, channels)
     pieces = len(chunk_tiles(channels // LANES))
+    peers = max(1, (tm_count - 1) // 2)
     bf16 = jnp.bfloat16
     any_spec = pl.BlockSpec(memory_space=pl.ANY)
     dma = pltpu.SemaphoreType.DMA
@@ -373,10 +516,19 @@
             pltpu.VMEM((rows * cols, extent * cols), jnp.float32),
             pltpu.VMEM((frames * cols, tm_count * frames * cols), jnp.float32),
             pltpu.SMEM(lists.shape[::-1], jnp.int32),
+            pltpu.VMEM((peers, frames, 1, cols, channels), bf16),
+            pltpu.VMEM((peers, frames, 1, cols, channels + LANES), bf16),
+            pltpu.VMEM((peers, frames, 1, cols, channels + LANES), bf16),
+            pltpu.VMEM((frames * cols, channels), jnp.float32),
+            pltpu.VMEM((LANES, channels), bf16),
             dma((2, pieces, 2 * reach)),
             dma((2, pieces, 2 * reach)),
             dma((2, pieces, tm_count)),
             dma((2, pieces, tm_count)),
+            dma((peers,)),
+            dma((peers,)),
+            dma((peers,)),
+            dma((peers,)),
             pltpu.SemaphoreType.REGULAR((max(reach, 1),)),
             pltpu.SemaphoreType.REGULAR((tm_count,)),
             dma((7,)),

time: 21 us -> 22 us (1.048)
  Pallas kernels: 20.2 us -> 21.2 us
    pallas_call x1, Pallas kernels: 19.3 us -> 20.4 us  [on_device(): pl.pallas_call(functools.partial(kernel, space_count, tm_count, reach), o...]
where the time goes in v2:
time: 22 us; the launch traced here: 21.8 us
  Pallas kernels  21.2 us (96%)
  between operations  0.64 us (3%)
    pallas_call x1, Pallas kernels, on_device(): pl.pallas_call(functools.partial(kernel, space_count, tm_count, reach), o...  20.4 us
    pallas_call x1, Pallas kernels, on_device(): pl.pallas_call(written, out_shape=(jax.ShapeDtypeStruct(block, bf16), jax...  0.83 us

profile of v2, /device:TPU:0, one launch (start us, length us, event | category | flops | bytes accessed | tf_op | source)
XLA Modules:
  0.0 21.8 jit_solution(5088607394673567912)
XLA Ops:
  0.6 20.4 %attention.1 = (bf16[2,4,16,1152]{3,2,1,0:T(8,128)(2,1)S(1)}, bf16[2,4,16,1152]{3,2,1,0:T(8,128)(2,1)S(1)}) custom-call(bf16[2,4,16,1152]{3,2,1,0:T(8,128)(2,1)} %sq.1, bf16[2,4,16,1152]{3,2,1,0:T(8,128)(2,1)} %sk.1, bf16[2,4,16,1152]{3,2,1,0:T(8,128)(2,1)} %sv.1, bf16[2,4,16,1152]{3,2,1,0:T(8,128)(2,1)} %tq.1, bf16[2,4,16,1152]{3,2,1,0:T(8,128)(2,1)} %tk.1, ...), custom_call_target="tpu_custom_call" | custom-call | tf_op jit(solution)/shard_map/attention/pallas_call | solution.py:504
  21.0 0.8 %written.1 = (bf16[2,4,16,1152]{3,2,1,0:T(8,128)(2,1)}, bf16[2,4,16,1152]{3,2,1,0:T(8,128)(2,1)}) custom-call(bf16[2,4,16,1152]{3,2,1,0:T(8,128)(2,1)S(1)} %get-tuple-element.4.first, bf16[2,4,16,1152]{3,2,1,0:T(8,128)(2,1)S(1)} %get-tuple-element.5.second), custom_call_target="tpu_custom_call" | custom-call | tf_op jit(solution)/shard_map/written/pallas_call | solution.py:539

commit v3 on v2

--- a/solution.py
+++ b/solution.py
@@ -29,7 +29,7 @@
     return groups
 
 
-CUTS = (5, 8)
+CUTS = (5, 7)
 
 
 def chunk_tiles(tiles):
@@ -384,6 +384,9 @@
         terms = jnp.where(lane < 2 * heads, second, jnp.where(lane < 3 * heads, third, none))
         return jnp.where(lane < heads, first, terms)
 
+    def spread_out(terms):
+        return jnp.dot(terms, spread[...], preferred_element_type=jnp.float32)
+
     def wait_direct(c):
         for j in direct[1:]:
             for which in (0, 1):
@@ -403,11 +406,17 @@
 
     ready = [[g for g in range(len(groups)) if needed_last[g] == c] for c in range(len(chunks))]
 
-    def across(c):
+    def across(c, beside=None):
         wait_z(c, 0)
+
+        def arrive():
+            if beside is not None:
+                beside(c)
+            wait_z(c, 1)
+
         for at in range(0, len(ready[c]), 2):
             problems = [spatial(g, f) for g in ready[c][at : at + 2] for f in range(frames)]
-            attend(problems, functools.partial(wait_z, c, 1) if at == 0 else None)
+            attend(problems, arrive if at == 0 else None)
 
     def along(c):
         wait_relayed(c)
@@ -426,32 +435,29 @@
         for n in range(len(lent)):
             terms = three(sums[n]).reshape(frames, 1, cols, LANES)
             answer[n, :, :, :, channels:] = terms
-        own_terms = three(sums[-1])
+        own_logs = spread_out(three(sums[-1]))
 
     def return_parts():
         for n in range(len(lent)):
             o_copy(n).start()
 
     last = len(chunks) - 1
-    for c in range(len(chunks)):
+    for c in range(last):
         wait_direct(c)
-        if c == max(last - 1, 0):
+        across(c)
+        if c == 0:
             return_parts()
-        if c < last - 1:
-            across(c)
-        if c == last and c > 0:
-            across(c - 1)
         along(c)
-    across(last)
+    wait_direct(last)
+    if last == 0:
+        return_parts()
+    across(last, along)
 
     if lent:
         for n in range(len(lent)):
             o_copy(n).wait_recv()
 
-        def spread_out(terms):
-            return jnp.dot(terms, spread[...], preferred_element_type=jnp.float32)
-
-        logs = [spread_out(own_terms)]
+        logs = [own_logs]
         parts = [own[...]]
         for n in range(len(lent)):
             logs.append(spread_out(answered[n, :, :, :, channels:].reshape(tokens, LANES)))

time: 22 us -> 20.2 us (0.918)
  Pallas kernels: 21.2 us -> 19.4 us
    pallas_call x1, Pallas kernels: 20.4 us -> 18.6 us  [on_device(): pl.pallas_call(functools.partial(kernel, space_count, tm_count, reach), o...]
where the time goes in v3:
time: 20.2 us; the launch traced here: 20 us
  Pallas kernels  19.4 us (96%)
  between operations  0.64 us (3%)
    pallas_call x1, Pallas kernels, on_device(): pl.pallas_call(functools.partial(kernel, space_count, tm_count, reach), o...  18.6 us
    pallas_call x1, Pallas kernels, on_device(): pl.pallas_call(written, out_shape=(jax.ShapeDtypeStruct(block, bf16), jax...  0.83 us

profile of v3, /device:TPU:0, one launch (start us, length us, event | category | flops | bytes accessed | tf_op | source)
XLA Modules:
  0.0 20.0 jit_solution(8793487644030852015)
XLA Ops:
  0.6 18.6 %attention.1 = (bf16[2,4,16,1152]{3,2,1,0:T(8,128)(2,1)S(1)}, bf16[2,4,16,1152]{3,2,1,0:T(8,128)(2,1)S(1)}) custom-call(bf16[2,4,16,1152]{3,2,1,0:T(8,128)(2,1)} %sq.1, bf16[2,4,16,1152]{3,2,1,0:T(8,128)(2,1)} %sk.1, bf16[2,4,16,1152]{3,2,1,0:T(8,128)(2,1)} %sv.1, bf16[2,4,16,1152]{3,2,1,0:T(8,128)(2,1)} %tq.1, bf16[2,4,16,1152]{3,2,1,0:T(8,128)(2,1)} %tk.1, ...), custom_call_target="tpu_custom_call" | custom-call | tf_op jit(solution)/shard_map/attention/pallas_call | solution.py:510
  19.2 0.8 %written.1 = (bf16[2,4,16,1152]{3,2,1,0:T(8,128)(2,1)}, bf16[2,4,16,1152]{3,2,1,0:T(8,128)(2,1)}) custom-call(bf16[2,4,16,1152]{3,2,1,0:T(8,128)(2,1)S(1)} %get-tuple-element.4.first, bf16[2,4,16,1152]{3,2,1,0:T(8,128)(2,1)S(1)} %get-tuple-element.5.second), custom_call_target="tpu_custom_call" | custom-call | tf_op jit(solution)/shard_map/written/pallas_call | solution.py:545
